TPU v7x, 256 devices: a whole 4x4x8 slice. The times are simulated.
256 devices in a mesh: ta: 4 (over y), ha: 16 (over x, z_hi, core), wa: 4 (over z_lo).
Axes of the slice: x: 4, y: 4, z: 8 (z_hi: 2, z_lo: 4; z = z_hi * 4 + z_lo), core: 2. Of those that a mesh axis runs over, the one named last changes fastest.
Arguments:
- latents: bfloat16 [8, 256, 128, 256], P('ta', 'ha', 'wa'), may hold values from -6 to 6
- norm_gain: float32 [256], replicated, may hold values from 0.1 to 1.9
- conv_weight: bfloat16 [3, 3, 3, 256, 256], replicated, may hold values from -0.078125 to 0.078125
- qkv_weight: bfloat16 [1024, 16, 3, 128], P(None, ('ta', 'wa')), may hold values from -2.7 to 2.7
Outputs:
- block_out: bfloat16 [8, 256, 128, 256], P('ta', 'ha', 'wa')
- attended: bfloat16 [8, 128, 64, 16, 128], P(None, 'ha', None, ('ta', 'wa'))
All inputs are finite; a program needn't handle non-finite values.
Results may differ from a plain program's by a relative error of at most 0.0062.
Values may be sent and summed in bfloat16 or wider, within the bound.
No kernel may reach another device: no remote copies, remote signals or barrier semaphores. Data moves between devices by JAX's collectives and lax.ppermute only.
A program may use at most 128 MiB of HBM per device.

v0:
```python
import jax
import jax.numpy as jnp
from jax import lax
from jax.sharding import PartitionSpec as P

WIN = 4


def extended(cells, sides, width):
    for axis, dim in sides:
        count = lax.axis_size(axis)
        ends = count - 1
        head = lax.slice_in_dim(cells, 0, width, axis=dim)
        tail = lax.slice_in_dim(cells, cells.shape[dim] - width, cells.shape[dim], axis=dim)
        cells = jnp.concatenate(
            [
                lax.ppermute(tail, axis, [(i, (i + 1) % count) for i in range(ends)]),
                cells,
                lax.ppermute(head, axis, [((i + 1) % count, i) for i in range(ends)]),
            ],
            axis=dim,
        )
    return cells


def local(latents, norm_gain, conv_weight, qkv_weight):
    t_dev, h_dev, w_dev, channels = latents.shape
    rows_dev = h_dev // 2
    cols_dev = w_dev // 2
    latent_f32 = latents.astype(jnp.float32)
    scale_rms = lax.rsqrt(jnp.mean(latent_f32 * latent_f32, axis=-1, keepdims=True) + 1e-06)
    normed = jax.nn.silu(latent_f32 * scale_rms * norm_gain).astype(jnp.bfloat16)
    padded = extended(normed, (("ta", 0), ("ha", 1), ("wa", 2)), 1)
    conv_out = lax.conv_general_dilated(
        padded[None],
        conv_weight,
        (1, 1, 1),
        "VALID",
        dimension_numbers=("NDHWC", "DHWIO", "NDHWC"),
        preferred_element_type=jnp.float32,
    )[0]
    block_out = (latent_f32 + conv_out).astype(jnp.bfloat16)
    patches = (
        block_out.reshape(t_dev, rows_dev, 2, cols_dev, 2, channels)
        .transpose(0, 1, 3, 2, 4, 5)
        .reshape(t_dev * rows_dev * cols_dev, 4 * channels)
    )
    width_in, head_dev, qkv_count, head_size = qkv_weight.shape
    every_head = lax.all_gather(qkv_weight, ("ta", "wa"), axis=1, tiled=True)
    projected = jnp.dot(
        patches, every_head.reshape(width_in, -1), preferred_element_type=jnp.float32
    ).astype(jnp.bfloat16)
    gathered = lax.all_to_all(projected, ("ta", "wa"), split_axis=1, concat_axis=0, tiled=True)
    n_time = lax.axis_size("ta")
    n_width = lax.axis_size("wa")
    frames = n_time * t_dev
    patch_cols = n_width * cols_dev
    qkv_rows = gathered.reshape(
        n_time, n_width, t_dev, rows_dev, cols_dev, head_dev, qkv_count, head_size
    )
    qkv_rows = qkv_rows.transpose(0, 2, 3, 1, 4, 5, 6, 7).reshape(
        frames, rows_dev, patch_cols, head_dev, qkv_count, head_size
    )
    queries = qkv_rows[:, :, :, :, 0, :]
    key_value = qkv_rows[:, :, :, :, 1:, :].reshape(
        frames, rows_dev, patch_cols, head_dev, 2 * head_size
    )
    kv_rim = extended(key_value, (("ha", 1),), WIN)
    row_base = lax.axis_index("ha") * rows_dev
    total_rows = rows_dev * lax.axis_size("ha")

    def attend(block_idx):
        q_block = lax.dynamic_slice_in_dim(queries, block_idx * WIN, WIN, 1)
        kv_block = lax.dynamic_slice_in_dim(kv_rim, block_idx * WIN, 3 * WIN, 1)
        key_part = kv_block[..., :head_size]
        value_part = kv_block[..., head_size:]
        scores = jnp.einsum(
            "tiahd,tjbhd->thiajb", q_block, key_part, preferred_element_type=jnp.float32
        ) * head_size ** (-0.5)
        q_row = jnp.arange(WIN, dtype=jnp.int32)[:, None]
        k_row = jnp.arange(3 * WIN, dtype=jnp.int32)[None, :] - WIN
        k_global = row_base + block_idx * WIN + k_row
        allowed = (jnp.abs(q_row - k_row) <= WIN) & (k_global >= 0) & (k_global < total_rows)
        scores = jnp.where(allowed[None, None, :, None, :, None], scores, -1e30)
        row_max = jnp.max(scores, axis=(4, 5), keepdims=True)
        exp_scores = jnp.exp(scores - row_max)
        probs = (exp_scores / jnp.sum(exp_scores, axis=(4, 5), keepdims=True)).astype(jnp.bfloat16)
        result = jnp.einsum(
            "thiajb,tjbhd->tiahd", probs, value_part, preferred_element_type=jnp.float32
        )
        return result.astype(jnp.bfloat16)

    blocks = lax.map(attend, jnp.arange(rows_dev // WIN, dtype=jnp.int32))
    attended = blocks.transpose(1, 0, 2, 3, 4, 5).reshape(
        frames, rows_dev, patch_cols, head_dev, head_size
    )
    return (block_out, attended)


def solution(mesh):
    return jax.shard_map(
        local,
        mesh=mesh,
        in_specs=(P("ta", "ha", "wa", None), P(), P(), P(None, ("ta", "wa"), None, None)),
        out_specs=(P("ta", "ha", "wa", None), P(None, "ha", None, ("ta", "wa"), None)),
        check_vma=False,
    )
```

profile of v0, /device:TPU:3, one launch (start us, length us, event | category | flops | bytes accessed | tf_op | source)
XLA Modules:
  0.0 499.1 jit_solution(14405158100643521824)
XLA Ops:
  7.9 1.7 fusion.27
  9.7 1.5 fusion.34
  11.2 3.2 collective-permute-start
  15.8 3.7 collective-permute-done
  19.4 3.8 collective-permute-done.1
  23.5 10.5 %collective-permute-start.2 = (bf16[4,1,32,256]{3,1,2,0:T(2,128)(2,1)S(1)}, bf16[4,1,32,256]{3,1,2,0:T(2,128)(2,1)S(1)}, u32[]{:S(2)}, u32[]{:S(2)}) collective-permute-start(bf16[4,1,32,256]{3,1,2,0:T(2,128)(2,1)S(1)} %get-tuple-element.106), channel_id=1, source_target_pairs={{0,4},{4,8},{8,12},{12,16},{16,20},{20,24},{24,28},{28,32},{32,36}... | collective-permute-start | bytes 196616 | tf_op jit(solution)/shard_map/ppermute | solution.py:17
  34.0 1.9 collective-permute-start.3
  35.9 4.1 collective-permute-done.2
  40.0 9.0 %collective-permute-done.3 = bf16[4,1,32,256]{3,1,2,0:T(2,128)(2,1)S(1)} collective-permute-done((bf16[4,1,32,256]{3,1,2,0:T(2,128)(2,1)S(1)}, bf16[4,1,32,256]{3,1,2,0:T(2,128)(2,1)S(1)}, u32[]{:S(2)}, u32[]{:S(2)}) %collective-permute-start.3) | collective-permute-done | bytes 65568 | tf_op jit(solution)/shard_map/ppermute | solution.py:19
  49.0 4.6 collective-permute-start.4
  55.9 6.5 %collective-permute-done.5 = bf16[4,18,1,256]{3,1,2,0:T(8,128)(2,1)S(1)} collective-permute-done((bf16[4,18,1,256]{3,1,2,0:T(8,128)(2,1)S(1)}, bf16[4,18,1,256]{3,1,2,0:T(8,128)(2,1)S(1)}, u32[]{:S(2)}, u32[]{:S(2)}) %collective-permute-start.5) | collective-permute-done | bytes 36896 | tf_op jit(solution)/shard_map/ppermute | solution.py:19
  65.2 5.0 %fusion.24 = f32[2,16,8,5,256]{4,2,3,1,0:T(8,128)S(1)} fusion(bf16[3,3,3,256,256]{4,3,2,1,0:T(8,128)(2,1)S(1)} %copy-done, bf16[4,18,1,7,2,256]{5,3,4,1,0,2:T(8,128)(2,1)S(1)} %slice.56, bf16[4,18,1,8,5,256]{5,3,4,1,0,2:T(8,128)(2,1)S(1)} %copy.38, pred[8,5]{0,1:T(8,128)(4,1)S(1)} %copy-done.8), kind=kOutput, calls=%fused_computation.42 | convolution fusion | flops 4536369152 | bytes 6840360 | tf_op jit(solution)/shard_map/conv_general_dilated | solution.py:34
  73.0 217.5 %all-gather.2.cloned.1.call-done = bf16[1024,16,3,128]{3,0,2,1:T(8,128)(2,1)} async-done(((bf16[1024,1,3,128]{3,0,2,1:T(8,128)(2,1)}), bf16[1024,16,3,128]{3,0,2,1:T(8,128)(2,1)}) %all-gather.2.cloned.1.call-update) | async-done | bytes 12582928 | tf_op jit(solution)/shard_map/all_gather | solution.py:49
  290.5 15.7 %copy.41 = bf16[1024,16,3,128]{0,3,2,1:T(8,128)(2,1)} copy(bf16[1024,16,3,128]{3,0,2,1:T(8,128)(2,1)} %all-gather.2.cloned.1.call-done) | data formatting | bytes 25165824 | tf_op jit(solution)/shard_map/all_gather | solution.py:49
  306.3 8.2 %convolution_convert_fusion = bf16[256,6144]{1,0:T(8,128)(2,1)S(1)} fusion(bf16[256,1024]{1,0:T(8,128)(2,1)} %reshape.155, bf16[1024,6144]{0,1:T(8,128)(2,1)} %bitcast.102), kind=kOutput, calls=%fused_computation.25 | convolution fusion | flops 3222798336 | bytes 16252928 | tf_op jit(solution)/shard_map/dot_general | solution.py:50
  315.0 76.1 %all_to_all.16 = bf16[256,16,384]{2,0,1:T(8,128)(2,1)S(1)} all-to-all(bf16[256,16,384]{2,0,1:T(8,128)(2,1)S(1)} %bitcast.105), channel_id=1, replica_groups=mesh['ta'=4,'ha'=16,'wa'=4] {'ta','wa'}, dimensions={1} | all-to-all | bytes 6291456 | tf_op jit(solution)/shard_map/all_to_all | solution.py:53
  391.1 3.9 reshape.157
  395.0 3.1 copy.43
  398.5 1.9 fusion.40
  400.4 8.9 %collective-permute-start.6 = (bf16[8,4,64,1,256]{4,2,1,0,3:T(8,128)(2,1)}, bf16[8,4,64,1,256]{4,2,1,0,3:T(8,128)(2,1)}, u32[]{:S(2)}, u32[]{:S(2)}) collective-permute-start(bf16[8,4,64,1,256]{4,2,1,0,3:T(8,128)(2,1)} %get-tuple-element.102), channel_id=1, source_target_pairs={{0,4},{4,8},{8,12},{12,16},{16,20},{20,24},{24,28},{28,32},{32,36}... | collective-permute-start | bytes 3145736 | tf_op jit(solution)/shard_map/ppermute | solution.py:17
  409.3 1.9 collective-permute-start.7
  413.5 37.9 %collective-permute-done.6 = bf16[8,4,64,1,256]{4,2,1,0,3:T(8,128)(2,1)} collective-permute-done((bf16[8,4,64,1,256]{4,2,1,0,3:T(8,128)(2,1)}, bf16[8,4,64,1,256]{4,2,1,0,3:T(8,128)(2,1)}, u32[]{:S(2)}, u32[]{:S(2)}) %collective-permute-start.6) | collective-permute-done | bytes 1048608 | tf_op jit(solution)/shard_map/ppermute | solution.py:17
  451.4 5.2 %collective-permute-done.7 = bf16[8,4,64,1,256]{4,2,1,0,3:T(8,128)(2,1)} collective-permute-done((bf16[8,4,64,1,256]{4,2,1,0,3:T(8,128)(2,1)}, bf16[8,4,64,1,256]{4,2,1,0,3:T(8,128)(2,1)}, u32[]{:S(2)}, u32[]{:S(2)}) %collective-permute-start.7) | collective-permute-done | bytes 1048608 | tf_op jit(solution)/shard_map/ppermute | solution.py:19
  456.7 3.4 pad_maximum_fusion
  460.1 29.8 %while.12 = (s32[]{:T(128)}, bf16[2,8,4,64,1,128]{5,3,2,1,4,0:T(8,128)(2,1)}, s32[2]{0:T(128)S(1)}, bf16[8,16,64,1,256]{4,2,1,0,3:T(8,128)(2,1)}, s32[]{:T(128)}...) while((s32[]{:T(128)}, ...), condition=%wide.region_4.5_spmd, body=%wide.region_1.4_spmd.sunk | while | flops 824439104 | bytes 37807656 | solution.py:93
  461.4 3.7 fusion.50
  465.1 3.4 fusion.51
  468.5 5.5 %fusion.52 = bf16[2,8,4,64,1,128]{5,3,2,1,4,0:T(8,128)(2,1)S(1)} fusion(bf16[2,8,4,64,1,128]{5,3,2,1,4,0:T(8,128)(2,1)S(1)} %copy-done.6, s32[]{:T(128)S(6)} %copy.66, f32[8,4,64,12,64]{2,4,3,1,0:T(8,128)S(1)} %get-tuple-element.153, f32[8,4,64]{2,1,0:T(4,128)S(1)} %fusion.51, f32[8,4,64]{2,1,0:T(4,128)S(1)} %get-tuple-element.154, ...), kind=kOutput, calls=%fused_computation.12.clone.1 | convolution fusion | flops 410779648 | bytes 14713356 | tf_op jit(solution)/shard_map/while/body/eval_jaxpr/thiajb,tjbhd->tiahd/dot_general | solution.py:88
  476.3 3.7 fusion.50
  480.0 3.4 fusion.51
  483.4 5.5 %fusion.52 = bf16[2,8,4,64,1,128]{5,3,2,1,4,0:T(8,128)(2,1)S(1)} fusion(bf16[2,8,4,64,1,128]{5,3,2,1,4,0:T(8,128)(2,1)S(1)} %copy-done.6, s32[]{:T(128)S(6)} %copy.66, f32[8,4,64,12,64]{2,4,3,1,0:T(8,128)S(1)} %get-tuple-element.153, f32[8,4,64]{2,1,0:T(4,128)S(1)} %fusion.51, f32[8,4,64]{2,1,0:T(4,128)S(1)} %get-tuple-element.154, ...), kind=kOutput, calls=%fused_computation.12.clone.1 | convolution fusion | flops 410779648 | bytes 14713356 | tf_op jit(solution)/shard_map/while/body/eval_jaxpr/thiajb,tjbhd->tiahd/dot_general | solution.py:88
  489.9 2.4 copy.45
  (55 shorter events, 16.3 us)
Async XLA Ops:
  7.2 58.0 %copy-start = (bf16[3,3,3,256,256]{4,3,2,1,0:T(8,128)(2,1)S(1)}, bf16[3,3,3,256,256]{4,3,2,1,0:T(8,128)(2,1)}, u32[]{:S(2)}) copy-start(bf16[3,3,3,256,256]{4,3,2,1,0:T(8,128)(2,1)} %param.8) | copy-start | bytes 10616836
  7.2 283.3 %all-gather.2.cloned.1.call-start = ((), (), s32[]{:S(2)}) async-start(), calls=%async_computation.1 | async-start | bytes 13369344 | tf_op jit(solution)/shard_map/all_gather | solution.py:49
  11.2 8.2 %collective-permute-start = (bf16[1,16,32,256]{3,1,2,0:T(8,128)(2,1)S(1)}, bf16[1,16,32,256]{3,1,2,0:T(8,128)(2,1)S(1)}, u32[]{:S(2)}, u32[]{:S(2)}) collective-permute-start(bf16[1,16,32,256]{3,1,2,0:T(8,128)(2,1)S(1)} %get-tuple-element.108), channel_id=1, source_target_pairs={{0,64},{64,128},{128,192},{1,65},{65,129},{129,193},{2,66},{66,130... | collective-permute-start | bytes 786440 | tf_op jit(solution)/shard_map/ppermute | solution.py:17
  14.5 8.8 %collective-permute-start.1 = (bf16[1,16,32,256]{3,1,2,0:T(8,128)(2,1)S(1)}, bf16[1,16,32,256]{3,1,2,0:T(8,128)(2,1)S(1)}, u32[]{:S(2)}, u32[]{:S(2)}) collective-permute-start(bf16[1,16,32,256]{3,1,2,0:T(8,128)(2,1)S(1)} %get-tuple-element.109), channel_id=1, source_target_pairs={{64,0},{128,64},{192,128},{65,1},{129,65},{193,129},{66,2},{130,66... | collective-permute-start | bytes 786440 | tf_op jit(solution)/shard_map/ppermute | solution.py:19
  23.5 16.5 %collective-permute-start.2 = (bf16[4,1,32,256]{3,1,2,0:T(2,128)(2,1)S(1)}, bf16[4,1,32,256]{3,1,2,0:T(2,128)(2,1)S(1)}, u32[]{:S(2)}, u32[]{:S(2)}) collective-permute-start(bf16[4,1,32,256]{3,1,2,0:T(2,128)(2,1)S(1)} %get-tuple-element.106), channel_id=1, source_target_pairs={{0,4},{4,8},{8,12},{12,16},{16,20},{20,24},{24,28},{28,32},{32,36}... | collective-permute-start | bytes 196616 | tf_op jit(solution)/shard_map/ppermute | solution.py:17
  34.0 15.0 %collective-permute-start.3 = (bf16[4,1,32,256]{3,1,2,0:T(2,128)(2,1)S(1)}, bf16[4,1,32,256]{3,1,2,0:T(2,128)(2,1)S(1)}, u32[]{:S(2)}, u32[]{:S(2)}) collective-permute-start(bf16[4,1,32,256]{3,1,2,0:T(2,128)(2,1)S(1)} %get-tuple-element.107), channel_id=1, source_target_pairs={{4,0},{8,4},{12,8},{16,12},{20,16},{24,20},{28,24},{32,28},{36,32}... | collective-permute-start | bytes 196616 | tf_op jit(solution)/shard_map/ppermute | solution.py:19
  49.0 6.8 %collective-permute-start.4 = (bf16[4,18,1,256]{3,1,2,0:T(8,128)(2,1)S(1)}, bf16[4,18,1,256]{3,1,2,0:T(8,128)(2,1)S(1)}, u32[]{:S(2)}, u32[]{:S(2)}) collective-permute-start(bf16[4,18,1,256]{3,1,2,0:T(8,128)(2,1)S(1)} %get-tuple-element.104), channel_id=1, source_target_pairs={{0,1},{1,2},{2,3},{4,5},{5,6},{6,7},{8,9},{9,10},{10,11},{12,13},{... | collective-permute-start | bytes 110600 | tf_op jit(solution)/shard_map/ppermute | solution.py:17
  53.7 8.7 %collective-permute-start.5 = (bf16[4,18,1,256]{3,1,2,0:T(8,128)(2,1)S(1)}, bf16[4,18,1,256]{3,1,2,0:T(8,128)(2,1)S(1)}, u32[]{:S(2)}, u32[]{:S(2)}) collective-permute-start(bf16[4,18,1,256]{3,1,2,0:T(8,128)(2,1)S(1)} %get-tuple-element.105), channel_id=1, source_target_pairs={{1,0},{2,1},{3,2},{5,4},{6,5},{7,6},{9,8},{10,9},{11,10},{13,12},{... | collective-permute-start | bytes 110600 | tf_op jit(solution)/shard_map/ppermute | solution.py:19
  64.1 1.1 copy-start.8
  65.2 5.4 %copy-start.3 = (bf16[2,16,32,256]{3,2,1,0:T(8,128)(2,1)S(1)}, bf16[2,16,32,256]{3,2,1,0:T(8,128)(2,1)}, u32[]{:S(2)}) copy-start(bf16[2,16,32,256]{3,2,1,0:T(8,128)(2,1)} %param.6) | copy-start | bytes 1572868
  71.1 235.2 %copy-start.4 = (bf16[2,16,32,256]{3,1,2,0:T(8,128)(2,1)}, bf16[2,16,32,256]{3,1,2,0:T(8,128)(2,1)S(1)}, u32[]{:S(2)}) copy-start(bf16[2,16,32,256]{3,1,2,0:T(8,128)(2,1)S(1)} %fusion.35) | copy-start | bytes 1572868
  398.0 2.4 copy-start.2
  398.1 13.2 %copy-start.5 = (bf16[2,16,32,256]{3,1,2,0:T(8,128)(2,1)S(1)}, bf16[2,16,32,256]{3,1,2,0:T(8,128)(2,1)}, u32[]{:S(2)}) copy-start(bf16[2,16,32,256]{3,1,2,0:T(8,128)(2,1)} %copy-done.4) | copy-start | bytes 1572868
  400.4 51.0 %collective-permute-start.6 = (bf16[8,4,64,1,256]{4,2,1,0,3:T(8,128)(2,1)}, bf16[8,4,64,1,256]{4,2,1,0,3:T(8,128)(2,1)}, u32[]{:S(2)}, u32[]{:S(2)}) collective-permute-start(bf16[8,4,64,1,256]{4,2,1,0,3:T(8,128)(2,1)} %get-tuple-element.102), channel_id=1, source_target_pairs={{0,4},{4,8},{8,12},{12,16},{16,20},{20,24},{24,28},{28,32},{32,36}... | collective-permute-start | bytes 3145736 | tf_op jit(solution)/shard_map/ppermute | solution.py:17
  409.3 47.4 %collective-permute-start.7 = (bf16[8,4,64,1,256]{4,2,1,0,3:T(8,128)(2,1)}, bf16[8,4,64,1,256]{4,2,1,0,3:T(8,128)(2,1)}, u32[]{:S(2)}, u32[]{:S(2)}) collective-permute-start(bf16[8,4,64,1,256]{4,2,1,0,3:T(8,128)(2,1)} %get-tuple-element.103), channel_id=1, source_target_pairs={{4,0},{8,4},{12,8},{16,12},{20,16},{24,20},{28,24},{32,28},{36,32}... | collective-permute-start | bytes 3145736 | tf_op jit(solution)/shard_map/ppermute | solution.py:19
  465.1 3.5 copy-start.6
  474.0 1.0 copy-start.7
  479.9 3.5 copy-start.6
  488.9 1.0 copy-start.7
  489.9 2.4 copy-start.1
Sparse Core Ops, SparseCore 0:
  9.8 280.7 all-gather.1
where the time goes:
time: 500 us; the launch traced here: 499 us
  waiting for transfers between devices  289 us (58%)
  blocking collectives  76.1 us (15%)
  local copies, waits for them, and re-layouts  37.4 us (7%)
  starting transfers between devices  33.7 us (7%)
  matrix products  31.5 us (6%)
  other arithmetic  15.3 us (3%)
  between operations  14.3 us (3%)
    all_gather x1, waiting for transfers between devices, local(): every_head = lax.all_gather(qkv_weight, ('ta', 'wa'), axis=1, tiled=True)  218 us
    all_to_all x1, blocking collectives, local(): lax.all_to_all(projected, ('ta', 'wa'), split_axis=1, concat_axis=0, tile...  76.1 us
    ppermute x4, waiting for transfers between devices, extended(): lax.ppermute(tail, axis, [(i, (i + 1) % count) for i in range(ends)])  46.5 us
    ppermute x4, starting transfers between devices, extended(): lax.ppermute(tail, axis, [(i, (i + 1) % count) for i in range(ends)])  27.3 us
    ppermute x4, waiting for transfers between devices, extended(): lax.ppermute(head, axis, [((i + 1) % count, i) for i in range(ends)])  24.6 us
    all_gather x1, local copies, waits for them, and re-layouts, local(): every_head = lax.all_gather(qkv_weight, ('ta', 'wa'), axis=1, tiled=True)  15.7 us
    dot_general x2, matrix products, attend(): jnp.einsum('thiajb,tjbhd->tiahd', probs, value_part, preferred_element_ty...  10.9 us
  transfers between devices with their start and end apart: 9, of which 9 were waited for; matrix products, arithmetic and copies ran while one was open for 3% of the time, Pallas kernels for 0%

commit v1 on v0

--- a/solution.py
+++ b/solution.py
@@ -4,6 +4,18 @@
 from jax.sharding import PartitionSpec as P
 
 WIN = 4
+
+
+def _meet_strings(w_in):
+    return jnp.concatenate(
+        lax.all_to_all(
+            jnp.stack([w_in for _ in range(lax.axis_size(("ta", "wa")))]),
+            axis_name=("ta", "wa"),
+            split_axis=0,
+            concat_axis=0,
+        ),
+        axis=1,
+    )
 
 
 def extended(cells, sides, width):
@@ -46,7 +58,7 @@
         .reshape(t_dev * rows_dev * cols_dev, 4 * channels)
     )
     width_in, head_dev, qkv_count, head_size = qkv_weight.shape
-    every_head = lax.all_gather(qkv_weight, ("ta", "wa"), axis=1, tiled=True)
+    every_head = _meet_strings(qkv_weight)
     projected = jnp.dot(
         patches, every_head.reshape(width_in, -1), preferred_element_type=jnp.float32
     ).astype(jnp.bfloat16)

time: 500 us -> 517 us (1.034)
  starting transfers between devices: 33.7 us -> 51.1 us
  between operations: 14.3 us -> 0.97 us
  matrix products: 31.5 us -> 42.7 us
  waiting for transfers between devices: 289 us -> 279 us
  blocking collectives: 76.1 us -> 85.7 us
    all_gather x1 -> x0, waiting for transfers between devices: 218 us -> none  [local(): every_head = lax.all_gather(qkv_weight, ('ta', 'wa'), axis=1, tiled=True)]
    ppermute x4, waiting for transfers between devices: 46.5 us -> 213 us  [extended(): lax.ppermute(tail, axis, [(i, (i + 1) % count) for i in range(ends)])]
    all_to_all x0 -> x1, waiting for transfers between devices: none -> 50.9 us  [_meet_strings(): lax.all_to_all(jnp.stack([w_in for _ in range(lax.axis_size(('ta', 'wa'))...]
    all_gather x1 -> x0, local copies, waits for them, and re-layouts: 15.7 us -> none  [local(): every_head = lax.all_gather(qkv_weight, ('ta', 'wa'), axis=1, tiled=True)]
    another operation x0 -> x2, local copies, waits for them, and re-layouts: none -> 9.68 us  [the longest x1 7.24 us: _meet_strings(): jnp.stack([w_in for _ in range(lax.axis_size(('ta', 'wa')))])]
    all_to_all x1, blocking collectives: 76.1 us -> 85.7 us  [local(): lax.all_to_all(projected, ('ta', 'wa'), split_axis=1, concat_axis=0, tile...]
    while x8 -> x12, local copies, waits for them, and re-layouts: 1.94 us -> 11 us
    ppermute x4, waiting for transfers between devices: 24.6 us -> 15.8 us  [extended(): lax.ppermute(head, axis, [((i + 1) % count, i) for i in range(ends)])]
  transfers between devices with their start and end apart: 9 -> 9, of which waited for: 9 -> 8; matrix products, arithmetic and copies ran while one was open for 3% -> 3% of each run, Pallas kernels for 0% -> 0%
where the time goes in v1:
time: 517 us; the launch traced here: 516 us
  waiting for transfers between devices  279 us (54%)
  blocking collectives  85.7 us (17%)
  starting transfers between devices  51.1 us (10%)
  matrix products  42.7 us (8%)
  local copies, waits for them, and re-layouts  39.6 us (8%)
  other arithmetic  14.9 us (3%)
    ppermute x4, waiting for transfers between devices, extended(): lax.ppermute(tail, axis, [(i, (i + 1) % count) for i in range(ends)])  213 us
    all_to_all x1, blocking collectives, local(): lax.all_to_all(projected, ('ta', 'wa'), split_axis=1, concat_axis=0, tile...  85.7 us
    all_to_all x1, waiting for transfers between devices, _meet_strings(): lax.all_to_all(jnp.stack([w_in for _ in range(lax.axis_size(('ta', 'wa'))...  50.9 us
    ppermute x4, starting transfers between devices, extended(): lax.ppermute(tail, axis, [(i, (i + 1) % count) for i in range(ends)])  36 us
    dot_general x2, matrix products, attend(): jnp.einsum('thiajb,tjbhd->tiahd', probs, value_part, preferred_element_ty...  17.2 us
    ppermute x4, waiting for transfers between devices, extended(): lax.ppermute(head, axis, [((i + 1) % count, i) for i in range(ends)])  15.8 us
    dot_general x1, matrix products, local(): jnp.dot(patches, every_head.reshape(width_in, -1), preferred_element_type...  13.1 us
    while x12, local copies, waits for them, and re-layouts  11 us
  transfers between devices with their start and end apart: 9, of which 8 were waited for; matrix products, arithmetic and copies ran while one was open for 3% of the time, Pallas kernels for 0%

profile of v1, /device:TPU:3, one launch (start us, length us, event | category | flops | bytes accessed | tf_op | source)
XLA Modules:
  0.0 515.8 jit_solution(1629433801327672550)
XLA Ops:
  0.6 2.4 copy.42
  3.1 7.2 %stack.2 = bf16[16,1024,1,3,128]{1,4,3,2,0:T(8,128)(2,1)} broadcast(bf16[1024,3,128]{0,2,1:T(8,128)(2,1)} %copy.42), dimensions={1,3,4} | broadcast | bytes 13369344 | tf_op jit(solution)/shard_map/stack | solution.py:12
  10.3 8.5 %all-to-all-start = ((bf16[16,1024,1,3,128]{1,4,3,2,0:T(8,128)(2,1)}), bf16[16,1024,1,3,128]{1,4,3,2,0:T(8,128)(2,1)}, u32[]{:S(2)}, u32[]{:S(2)}) async-start(bf16[16,1024,1,3,128]{1,4,3,2,0:T(8,128)(2,1)} %stack.2), calls=%async_computation | async-start | bytes 25165824 | tf_op jit(solution)/shard_map/all_to_all | solution.py:11
  21.9 3.2 collective-permute-start
  26.4 115.5 %collective-permute-done = bf16[1,16,32,256]{3,1,2,0:T(8,128)(2,1)S(1)} collective-permute-done((bf16[1,16,32,256]{3,1,2,0:T(8,128)(2,1)S(1)}, bf16[1,16,32,256]{3,1,2,0:T(8,128)(2,1)S(1)}, u32[]{:S(2)}, u32[]{:S(2)}) %collective-permute-start) | collective-permute-done | bytes 262176 | tf_op jit(solution)/shard_map/ppermute | solution.py:29
  141.9 2.9 collective-permute-done.1
  145.0 23.8 %collective-permute-start.2 = (bf16[4,1,32,256]{3,1,2,0:T(2,128)(2,1)S(1)}, bf16[4,1,32,256]{3,1,2,0:T(2,128)(2,1)S(1)}, u32[]{:S(2)}, u32[]{:S(2)}) collective-permute-start(bf16[4,1,32,256]{3,1,2,0:T(2,128)(2,1)S(1)} %get-tuple-element.106), channel_id=1, source_target_pairs={{0,4},{4,8},{8,12},{12,16},{16,20},{20,24},{24,28},{28,32},{32,36}... | collective-permute-start | bytes 196616 | tf_op jit(solution)/shard_map/ppermute | solution.py:29
  170.7 56.9 %collective-permute-done.2 = bf16[4,1,32,256]{3,1,2,0:T(2,128)(2,1)S(1)} collective-permute-done((bf16[4,1,32,256]{3,1,2,0:T(2,128)(2,1)S(1)}, bf16[4,1,32,256]{3,1,2,0:T(2,128)(2,1)S(1)}, u32[]{:S(2)}, u32[]{:S(2)}) %collective-permute-start.2) | collective-permute-done | bytes 65568 | tf_op jit(solution)/shard_map/ppermute | solution.py:29
  227.6 5.8 %collective-permute-done.3 = bf16[4,1,32,256]{3,1,2,0:T(2,128)(2,1)S(1)} collective-permute-done((bf16[4,1,32,256]{3,1,2,0:T(2,128)(2,1)S(1)}, bf16[4,1,32,256]{3,1,2,0:T(2,128)(2,1)S(1)}, u32[]{:S(2)}, u32[]{:S(2)}) %collective-permute-start.3) | collective-permute-done | bytes 65568 | tf_op jit(solution)/shard_map/ppermute | solution.py:31
  236.2 3.3 collective-permute-done.5
  242.4 5.0 fusion.24
  249.4 50.9 %all-to-all-done = bf16[16,1024,1,3,128]{1,4,3,2,0:T(8,128)(2,1)} async-done(((bf16[16,1024,1,3,128]{1,4,3,2,0:T(8,128)(2,1)}), bf16[16,1024,1,3,128]{1,4,3,2,0:T(8,128)(2,1)}, u32[]{:S(2)}, u32[]{:S(2)}) %all-to-all-start) | async-done | bytes 12582944 | tf_op jit(solution)/shard_map/all_to_all | solution.py:11
  300.3 13.1 %convolution_convert_fusion = bf16[256,6144]{1,0:T(8,128)(2,1)S(1)} fusion(bf16[256,1024]{1,0:T(8,128)(2,1)S(1)} %reshape.158, bf16[1024,6144]{0,1:T(8,128)(2,1)} %bitcast.24), kind=kOutput, calls=%fused_computation.25 | convolution fusion | flops 3222798336 | bytes 16252928 | tf_op jit(solution)/shard_map/dot_general | solution.py:62
  314.0 85.7 %all_to_all.21 = bf16[256,16,384]{2,0,1:T(8,128)(2,1)S(1)} all-to-all(bf16[256,16,384]{2,0,1:T(8,128)(2,1)S(1)} %bitcast.109), channel_id=1, replica_groups=mesh['ta'=4,'ha'=16,'wa'=4] {'ta','wa'}, dimensions={1} | all-to-all | bytes 6291456 | tf_op jit(solution)/shard_map/all_to_all | solution.py:65
  399.7 3.8 reshape.160
  403.5 3.1 copy.45
  407.1 1.9 fusion.40
  409.0 7.7 %collective-permute-start.6 = (bf16[8,4,64,1,256]{4,2,1,0,3:T(8,128)(2,1)}, bf16[8,4,64,1,256]{4,2,1,0,3:T(8,128)(2,1)}, u32[]{:S(2)}, u32[]{:S(2)}) collective-permute-start(bf16[8,4,64,1,256]{4,2,1,0,3:T(8,128)(2,1)} %get-tuple-element.102), channel_id=1, source_target_pairs={{0,4},{4,8},{8,12},{12,16},{16,20},{20,24},{24,28},{28,32},{32,36}... | collective-permute-start | bytes 3145736 | tf_op jit(solution)/shard_map/ppermute | solution.py:29
  416.7 1.9 collective-permute-start.7
  420.9 40.2 %collective-permute-done.6 = bf16[8,4,64,1,256]{4,2,1,0,3:T(8,128)(2,1)} collective-permute-done((bf16[8,4,64,1,256]{4,2,1,0,3:T(8,128)(2,1)}, bf16[8,4,64,1,256]{4,2,1,0,3:T(8,128)(2,1)}, u32[]{:S(2)}, u32[]{:S(2)}) %collective-permute-start.6) | collective-permute-done | bytes 1048608 | tf_op jit(solution)/shard_map/ppermute | solution.py:29
  461.2 3.8 collective-permute-done.7
  465.0 3.4 pad_maximum_fusion
  468.3 45.0 %while.12 = (s32[]{:T(128)}, bf16[2,8,4,64,1,128]{5,3,2,1,4,0:T(8,128)(2,1)}, s32[2]{0:T(128)S(1)}, bf16[8,16,64,1,256]{4,2,1,0,3:T(8,128)(2,1)}, s32[]{:T(128)}...) while((s32[]{:T(128)}, ...), condition=%wide.region_4.5_spmd, body=%wide.region_1.4_spmd.sunk | while | flops 824439104 | bytes 62974008 | solution.py:105
  469.6 3.7 fusion.50
  473.4 4.5 copy-done.2
  477.9 3.4 fusion.51
  481.3 8.6 %fusion.52 = bf16[2,8,4,64,1,128]{5,3,2,1,4,0:T(8,128)(2,1)S(1)} fusion(bf16[2,8,4,64,1,128]{5,3,2,1,4,0:T(8,128)(2,1)S(1)} %copy-done.7, s32[]{:T(128)} %get-tuple-element.167, f32[8,4,64,12,64]{2,4,3,1,0:T(8,128)} %copy-done.2, f32[8,4,64]{2,1,0:T(4,128)S(1)} %fusion.51, f32[8,4,64]{2,1,0:T(4,128)S(1)} %get-tuple-element.154, ...), kind=kOutput, calls=%fused_computation.12.clone.1 | convolution fusion | flops 410779648 | bytes 14713864 | tf_op jit(solution)/shard_map/while/body/eval_jaxpr/thiajb,tjbhd->tiahd/dot_general | solution.py:100
  492.2 3.7 fusion.50
  495.9 4.5 copy-done.2
  500.4 3.4 fusion.51
  503.8 8.6 %fusion.52 = bf16[2,8,4,64,1,128]{5,3,2,1,4,0:T(8,128)(2,1)S(1)} fusion(bf16[2,8,4,64,1,128]{5,3,2,1,4,0:T(8,128)(2,1)S(1)} %copy-done.7, s32[]{:T(128)} %get-tuple-element.167, f32[8,4,64,12,64]{2,4,3,1,0:T(8,128)} %copy-done.2, f32[8,4,64]{2,1,0:T(4,128)S(1)} %fusion.51, f32[8,4,64]{2,1,0:T(4,128)S(1)} %get-tuple-element.154, ...), kind=kOutput, calls=%fused_computation.12.clone.1 | convolution fusion | flops 410779648 | bytes 14713864 | tf_op jit(solution)/shard_map/while/body/eval_jaxpr/thiajb,tjbhd->tiahd/dot_general | solution.py:100
  513.4 2.4 copy.47
  (61 shorter events, 20.3 us)
Async XLA Ops:
  0.6 241.7 %copy-start = (bf16[3,3,3,256,256]{4,3,2,1,0:T(8,128)(2,1)S(1)}, bf16[3,3,3,256,256]{4,3,2,1,0:T(8,128)(2,1)}, u32[]{:S(2)}) copy-start(bf16[3,3,3,256,256]{4,3,2,1,0:T(8,128)(2,1)} %param.8) | copy-start | bytes 10616836
  10.3 10.0 %copy-start.9 = (f32[256]{0:T(256)S(1)}, f32[256]{0:T(256)}, u32[]{:S(2)}) copy-start(f32[256]{0:T(256)} %param.7) | copy-start | bytes 3076
  10.3 290.0 %all-to-all-start = ((bf16[16,1024,1,3,128]{1,4,3,2,0:T(8,128)(2,1)}), bf16[16,1024,1,3,128]{1,4,3,2,0:T(8,128)(2,1)}, u32[]{:S(2)}, u32[]{:S(2)}) async-start(bf16[16,1024,1,3,128]{1,4,3,2,0:T(8,128)(2,1)} %stack.2), calls=%async_computation | async-start | bytes 25165824 | tf_op jit(solution)/shard_map/all_to_all | solution.py:11
  21.9 120.0 %collective-permute-start = (bf16[1,16,32,256]{3,1,2,0:T(8,128)(2,1)S(1)}, bf16[1,16,32,256]{3,1,2,0:T(8,128)(2,1)S(1)}, u32[]{:S(2)}, u32[]{:S(2)}) collective-permute-start(bf16[1,16,32,256]{3,1,2,0:T(8,128)(2,1)S(1)} %get-tuple-element.108), channel_id=1, source_target_pairs={{0,64},{64,128},{128,192},{1,65},{65,129},{129,193},{2,66},{66,130... | collective-permute-start | bytes 786440 | tf_op jit(solution)/shard_map/ppermute | solution.py:29
  25.1 119.6 %collective-permute-start.1 = (bf16[1,16,32,256]{3,1,2,0:T(8,128)(2,1)S(1)}, bf16[1,16,32,256]{3,1,2,0:T(8,128)(2,1)S(1)}, u32[]{:S(2)}, u32[]{:S(2)}) collective-permute-start(bf16[1,16,32,256]{3,1,2,0:T(8,128)(2,1)S(1)} %get-tuple-element.109), channel_id=1, source_target_pairs={{64,0},{128,64},{192,128},{65,1},{129,65},{193,129},{66,2},{130,66... | collective-permute-start | bytes 786440 | tf_op jit(solution)/shard_map/ppermute | solution.py:31
  145.0 82.6 %collective-permute-start.2 = (bf16[4,1,32,256]{3,1,2,0:T(2,128)(2,1)S(1)}, bf16[4,1,32,256]{3,1,2,0:T(2,128)(2,1)S(1)}, u32[]{:S(2)}, u32[]{:S(2)}) collective-permute-start(bf16[4,1,32,256]{3,1,2,0:T(2,128)(2,1)S(1)} %get-tuple-element.106), channel_id=1, source_target_pairs={{0,4},{4,8},{8,12},{12,16},{16,20},{20,24},{24,28},{28,32},{32,36}... | collective-permute-start | bytes 196616 | tf_op jit(solution)/shard_map/ppermute | solution.py:29
  168.7 64.6 %collective-permute-start.3 = (bf16[4,1,32,256]{3,1,2,0:T(2,128)(2,1)S(1)}, bf16[4,1,32,256]{3,1,2,0:T(2,128)(2,1)S(1)}, u32[]{:S(2)}, u32[]{:S(2)}) collective-permute-start(bf16[4,1,32,256]{3,1,2,0:T(2,128)(2,1)S(1)} %get-tuple-element.107), channel_id=1, source_target_pairs={{4,0},{8,4},{12,8},{16,12},{20,16},{24,20},{28,24},{32,28},{36,32}... | collective-permute-start | bytes 196616 | tf_op jit(solution)/shard_map/ppermute | solution.py:31
  233.4 2.8 collective-permute-start.4
  234.7 4.8 collective-permute-start.5
  241.3 1.1 copy-start.10
  242.4 5.4 %copy-start.4 = (bf16[2,16,32,256]{3,2,1,0:T(8,128)(2,1)S(1)}, bf16[2,16,32,256]{3,2,1,0:T(8,128)(2,1)}, u32[]{:S(2)}) copy-start(bf16[2,16,32,256]{3,2,1,0:T(8,128)(2,1)} %param.6) | copy-start | bytes 1572868
  248.3 65.2 %copy-start.5 = (bf16[2,16,32,256]{3,1,2,0:T(8,128)(2,1)}, bf16[2,16,32,256]{3,1,2,0:T(8,128)(2,1)S(1)}, u32[]{:S(2)}) copy-start(bf16[2,16,32,256]{3,1,2,0:T(8,128)(2,1)S(1)} %fusion.35) | copy-start | bytes 1572868
  406.6 2.4 copy-start.3
  406.6 12.0 %copy-start.6 = (bf16[2,16,32,256]{3,1,2,0:T(8,128)(2,1)S(1)}, bf16[2,16,32,256]{3,1,2,0:T(8,128)(2,1)}, u32[]{:S(2)}) copy-start(bf16[2,16,32,256]{3,1,2,0:T(8,128)(2,1)} %copy-done.5) | copy-start | bytes 1572868
  409.0 52.2 %collective-permute-start.6 = (bf16[8,4,64,1,256]{4,2,1,0,3:T(8,128)(2,1)}, bf16[8,4,64,1,256]{4,2,1,0,3:T(8,128)(2,1)}, u32[]{:S(2)}, u32[]{:S(2)}) collective-permute-start(bf16[8,4,64,1,256]{4,2,1,0,3:T(8,128)(2,1)} %get-tuple-element.102), channel_id=1, source_target_pairs={{0,4},{4,8},{8,12},{12,16},{16,20},{20,24},{24,28},{28,32},{32,36}... | collective-permute-start | bytes 3145736 | tf_op jit(solution)/shard_map/ppermute | solution.py:29
  416.7 48.3 %collective-permute-start.7 = (bf16[8,4,64,1,256]{4,2,1,0,3:T(8,128)(2,1)}, bf16[8,4,64,1,256]{4,2,1,0,3:T(8,128)(2,1)}, u32[]{:S(2)}, u32[]{:S(2)}) collective-permute-start(bf16[8,4,64,1,256]{4,2,1,0,3:T(8,128)(2,1)} %get-tuple-element.103), channel_id=1, source_target_pairs={{4,0},{8,4},{12,8},{16,12},{20,16},{24,20},{28,24},{32,28},{36,32}... | collective-permute-start | bytes 3145736 | tf_op jit(solution)/shard_map/ppermute | solution.py:31
  473.3 4.5 copy-start.2
  477.9 3.4 copy-start.7
  489.9 1.0 copy-start.8
  495.9 4.5 copy-start.2
  500.4 3.4 copy-start.7
  512.4 1.0 copy-start.8
  513.4 2.4 copy-start.1
